TPU v7x, 32 devices: a whole 2x2x4 slice. The times are simulated.
32 devices in a mesh: ty: 4 (over x, core), tx: 8 (over z, y).
Axes of the slice: x: 2, y: 2, z: 4, core: 2. Of those that a mesh axis runs over, the one named last changes fastest.
Arguments:
- intensity: float32 [64, 256, 256], P(('ty', 'tx')), may hold values from 0 to 3
- corner: int32 [64, 2], P(('ty', 'tx')), may hold values from 0 to 768, as said below
- probe: float32 [2, 256, 256], replicated, may hold values from -6 to 6
- prop_phase: float32 [256, 256], replicated, may hold values from -3.140625 to 3.140625
- object_slices: float32 [2, 2, 1024, 1024], P(None, None, 'ty', 'tx'), may hold values from -5 to 5
- momentum: float32 [2, 2, 1024, 1024], P(None, None, 'ty', 'tx'), may hold values from -6 to 6
Outputs:
- object_next: float32 [2, 2, 1024, 1024], P(None, None, 'ty', 'tx')
- momentum_next: float32 [2, 2, 1024, 1024], P(None, None, 'ty', 'tx')
Inputs may be any that keep to these rules, and one draw needn't show every extreme that they name: `corner`: patch p belongs to device p // 2 of ty+tx (ty slowest); with t = p // (2 times the size of tx) and s = (p // 2) modulo the size of tx, its row offset lies between max(t * 256 - 256 / 2, 0) and min(t * 256 + 256 - 256 / 2, 768), and its column offset between max(s * 128 - 256 / 2, 0) and min(s * 128 + 128 - 256 / 2, 768).
All inputs are finite; a program needn't handle non-finite values.
Results may differ from a plain program's by a relative error of at most 0.0003.
Values sent between devices are 32-bit elements; how exact they have to be, the bound alone decides.
A program may use at most 64 MiB of HBM per device.

v0:
```python
import functools
import math

import jax
import jax.numpy as jnp
import numpy as np
from jax import lax
from jax.experimental import pallas as pl
from jax.experimental.pallas import tpu as pltpu
from jax.sharding import PartitionSpec as P

decay_rate = 0.9
grad_scale = 0.05
step_length = 0.5

VMEM = pl.BlockSpec(memory_space=pltpu.VMEM)
SMEM = pl.BlockSpec(memory_space=pltpu.SMEM)


def dft_tables(n):
    k = np.arange(n)
    angle = 2.0 * math.pi * (np.outer(k, k) % n) / n
    c, s = np.cos(angle) / math.sqrt(n), -np.sin(angle) / math.sqrt(n)
    right = np.block([[c, s], [-s, c]]).astype(np.float32)
    left = np.concatenate([c, s], axis=0).astype(np.float32)

    def split(t):
        hi = t.astype(jnp.bfloat16)
        lo = (t - hi.astype(np.float32)).astype(jnp.bfloat16)
        return hi, lo

    rh, rl = split(right)
    lh, ll = split(left)
    return (
        jnp.asarray(np.concatenate([rh, rh, rl], axis=0)),
        jnp.asarray(np.concatenate([lh, lh, ll], axis=1)),
    )


def halves(x):
    hi = x.astype(jnp.bfloat16)
    lo = (x - hi.astype(jnp.float32)).astype(jnp.bfloat16)
    return hi, lo


def fft2(xr, xi, right_ref, left_ref):
    n = xr.shape[-1]
    hi, lo = halves(jnp.concatenate([xr, xi], axis=1))
    y = jnp.dot(
        jnp.concatenate([hi, lo, hi], axis=1), right_ref[...], preferred_element_type=jnp.float32
    )
    hi, lo = halves(y)
    z = jnp.dot(
        left_ref[...], jnp.concatenate([hi, lo, hi], axis=0), preferred_element_type=jnp.float32
    )
    return z[:n, :n] - z[n:, n:], z[:n, n:] + z[n:, :n]


def ifft2(xr, xi, right_ref, left_ref):
    yi, yr = fft2(xi, xr, right_ref, left_ref)
    return yr, yi


def mul(ar, ai, br, bi):
    return ar * br - ai * bi, ar * bi + ai * br


def masks(sc_ref, p, n):
    r, c, odd = sc_ref[p, 0], sc_ref[p, 1], sc_ref[p, 2]
    h = n // 2
    rows = lax.broadcasted_iota(jnp.int32, (n, h), 0)
    cols = lax.broadcasted_iota(jnp.int32, (n, h), 1)
    later = (cols >= c).astype(jnp.int32)
    return rows >= r, (later + odd) == 1


def window(q, p, sc_ref, tiles, above_ref, below_ref, n):
    h = n // 2
    row_first, use_far = masks(sc_ref, p, n)
    cols = []
    for t, tile in enumerate(tiles):
        top = jnp.where(row_first[:h], above_ref[t, q], tile[q, h:, :])
        bottom = jnp.where(row_first[h:], tile[q, :h, :], below_ref[t, q])
        cols.append(jnp.concatenate([top, bottom], axis=0))
    own, partner, far = cols
    return jnp.concatenate([jnp.where(use_far, far, partner), own], axis=1)


def scatter(g, q, p, sc_ref, tiles, above_ref, below_ref, n):
    h = n // 2
    row_first, use_far = masks(sc_ref, p, n)
    left, own = g[:, :h], g[:, h:]
    zero = jnp.zeros_like(left)
    parts = (own, jnp.where(use_far, zero, left), jnp.where(use_far, left, zero))
    for t, (tile, v) in enumerate(zip(tiles, parts)):
        low = jnp.where(row_first, v, zero)
        high = jnp.where(row_first, zero, v)
        above_ref[t, q] += low[:h]
        tile[q, h:, :] += high[:h]
        tile[q, :h, :] += low[h:]
        below_ref[t, q] += high[h:]


def first_kernel(sc_ref, probe_ref, tr_ref, right_ref, left_ref, own, partner, far, above_ref, below_ref, phi_ref, roll_ref):
    n = probe_ref.shape[-1]

    def body(p, carry):
        r, c = lax.rem(sc_ref[p, 0], n), sc_ref[p, 1]
        pr = pltpu.roll(pltpu.roll(probe_ref[0], c, 1), r, 0)
        pi = pltpu.roll(pltpu.roll(probe_ref[1], c, 1), r, 0)
        roll_ref[p, 0] = pr
        roll_ref[p, 1] = pi
        tiles = (own, partner, far)
        wr = window(0, p, sc_ref, tiles, above_ref, below_ref, n)
        wi = window(1, p, sc_ref, tiles, above_ref, below_ref, n)
        xr, xi = fft2(*mul(pr, pi, wr, wi), right_ref, left_ref)
        xr, xi = ifft2(*mul(tr_ref[0], tr_ref[1], xr, xi), right_ref, left_ref)
        phi_ref[p, 0] = xr
        phi_ref[p, 1] = xi
        return carry

    lax.fori_loop(0, phi_ref.shape[0], body, 0)


def clear(refs):
    for ref in refs:
        ref[...] = jnp.zeros_like(ref)


def second_kernel(sc_ref, phi_ref, intensity_ref, right_ref, left_ref, own, partner, far, above_ref, below_ref, back_ref, g_own, g_partner, g_far, g_above, g_below):
    n = intensity_ref.shape[-1]
    clear((g_own, g_partner, g_far, g_above, g_below))

    def body(p, carry):
        tiles = (own, partner, far)
        wr = window(0, p, sc_ref, tiles, above_ref, below_ref, n)
        wi = window(1, p, sc_ref, tiles, above_ref, below_ref, n)
        pr, pi = phi_ref[p, 0], phi_ref[p, 1]
        fr, fi = fft2(*mul(pr, pi, wr, wi), right_ref, left_ref)
        res = 2.0 * (fr * fr + fi * fi - intensity_ref[p])
        br, bi = ifft2(res * fr, res * fi, right_ref, left_ref)
        zr, zi = mul(wr, -wi, br, bi)
        back_ref[p, 0] = zr
        back_ref[p, 1] = zi
        gr, gi = mul(phi_ref[p, 0], -phi_ref[p, 1], br, bi)
        outs = (g_own, g_partner, g_far)
        scatter(gr, 0, p, sc_ref, outs, g_above, g_below, n)
        scatter(gi, 1, p, sc_ref, outs, g_above, g_below, n)
        return carry

    lax.fori_loop(0, phi_ref.shape[0], body, 0)


def third_kernel(sc_ref, back_ref, roll_ref, tr_ref, right_ref, left_ref, g_own, g_partner, g_far, g_above, g_below):
    n = back_ref.shape[-1]
    clear((g_own, g_partner, g_far, g_above, g_below))

    def body(p, carry):
        xr, xi = fft2(back_ref[p, 0], back_ref[p, 1], right_ref, left_ref)
        xr, xi = ifft2(*mul(tr_ref[0], -tr_ref[1], xr, xi), right_ref, left_ref)
        gr, gi = mul(roll_ref[p, 0], -roll_ref[p, 1], xr, xi)
        outs = (g_own, g_partner, g_far)
        scatter(gr, 0, p, sc_ref, outs, g_above, g_below, n)
        scatter(gi, 1, p, sc_ref, outs, g_above, g_below, n)
        return carry

    lax.fori_loop(0, back_ref.shape[0], body, 0)


def call(kernel, outs, args, flops):
    return pl.pallas_call(
        kernel,
        out_shape=[jax.ShapeDtypeStruct(s, jnp.float32) for s in outs],
        in_specs=[SMEM] + [VMEM] * (len(args) - 1),
        out_specs=[VMEM] * len(outs),
        compiler_params=pltpu.CompilerParams(vmem_limit_bytes=48 << 20),
        cost_estimate=pl.CostEstimate(flops=flops, bytes_accessed=8 << 20, transcendentals=0),
    )(*args)


def on_device(intensity, corner, probe, prop_phase, object_slices, momentum):
    count, n = intensity.shape[0], intensity.shape[-1]
    h = n // 2
    _, _, tile_rows, tile_cols = object_slices.shape
    assert tile_rows == n and tile_cols == h
    nty, ntx = lax.axis_size("ty"), lax.axis_size("tx")
    assert ntx % 2 == 0
    iy, ix = lax.axis_index("ty"), lax.axis_index("tx")
    odd = ix % 2
    sc = jnp.stack(
        [
            corner[:, 0] - (iy * tile_rows - h),
            corner[:, 1] - (ix * tile_cols - h),
            jnp.full((count,), odd, jnp.int32),
        ],
        axis=1,
    )
    swap = [(i, i ^ 1) for i in range(ntx)]
    even_up = [(i, i + 2) for i in range(0, ntx - 2, 2)]
    odd_down = [(i + 2, i) for i in range(1, ntx - 2, 2)]
    relay = even_up + odd_down
    back = [(j, i) for i, j in relay]
    down = [(i, i + 1) for i in range(nty - 1)]
    up = [(i + 1, i) for i in range(nty - 1)]

    def halo(s):
        own = object_slices[s]
        partner = lax.ppermute(own, "tx", swap)
        far = lax.ppermute(partner, "tx", relay)
        above = lax.ppermute(jnp.stack([t[:, h:] for t in (own, partner, far)]), "ty", down)
        below = lax.ppermute(jnp.stack([t[:, :h] for t in (own, partner, far)]), "ty", up)
        return own, partner, far, above, below

    def fold(own, partner, far, above, below):
        from_below = lax.ppermute(above, "ty", up)
        from_above = lax.ppermute(below, "ty", down)

        def rows(tile, t):
            return tile + jnp.concatenate([from_above[t], from_below[t]], axis=1)

        far_in = lax.ppermute(rows(far, 2), "tx", back)
        partner_in = lax.ppermute(rows(partner, 1) + far_in, "tx", swap)
        return rows(own, 0) + partner_in

    right, left = dft_tables(n)
    transfer = jnp.stack([jnp.cos(prop_phase), jnp.sin(prop_phase)])
    field = (count, 2, n, n)
    bands = [(2, n, h)] * 3 + [(3, 2, h, h)] * 2
    flops = 2 * 48 * count * n * n * n
    halo_first = halo(0)
    halo_second = halo(1)
    phi, rolled = call(first_kernel, [field, field], (sc, probe, transfer, right, left) + halo_first, flops)
    back_wave, *bands_second = call(
        second_kernel, [field] + bands, (sc, phi, intensity, right, left) + halo_second, flops
    )
    bands_first = call(third_kernel, bands, (sc, back_wave, rolled, transfer, right, left), flops)
    grad_second = fold(*bands_second)
    grad_first = fold(*bands_first)
    gradient = jnp.stack([grad_first, grad_second])
    momentum_next = decay_rate * momentum + grad_scale * gradient
    object_next = object_slices - step_length * momentum_next
    return (object_next, momentum_next)


def solution(mesh):
    return jax.shard_map(
        on_device,
        mesh=mesh,
        in_specs=(
            P(("ty", "tx"), None, None),
            P(("ty", "tx"), None),
            P(),
            P(),
            P(None, None, "ty", "tx"),
            P(None, None, "ty", "tx"),
        ),
        out_specs=(P(None, None, "ty", "tx"), P(None, None, "ty", "tx")),
        check_vma=False,
    )
```

profile of v0, /device:TPU:6, one launch (start us, length us, event | category | flops | bytes accessed | tf_op | source)
XLA Modules:
  0.0 95.5 jit_solution(3389386823068927528)
XLA Ops:
  0.6 1.1 %slice_bitcast_fusion = (f32[2,256,128]{2,1,0:T(8,128)S(1)}, f32[2,256,128]{2,1,0:T(8,128)S(1)}) fusion(f32[2,2,256,128]{3,2,1,0:T(8,128)} %param.12), kind=kLoop, calls=%fused_computation.20 | loop fusion | bytes 1048576 | tf_op jit(solution)/shard_map/squeeze | solution.py:207
  1.8 0.6 collective-permute-start.4
  2.3 1.5 %collective-permute-start = (f32[2,256,128]{2,1,0:T(8,128)S(1)}, f32[2,256,128]{2,1,0:T(8,128)S(1)}, u32[]{:S(2)}, u32[]{:S(2)}) collective-permute-start(f32[2,256,128]{2,1,0:T(8,128)S(1)} %get-tuple-element.31.own), channel_id=1, source_target_pairs={{0,1},{1,0},{2,3},{3,2},{4,5},{5,4},{6,7},{7,6},{8,9},{9,8},{10,11... | collective-permute-start | bytes 786440 | tf_op jit(solution)/shard_map/ppermute | solution.py:208
  4.1 0.1 add_add_fusion.sc_ref
  4.1 0.9 cosine_bitcast_fusion
  5.1 10.4 %collective-permute-done.partner = f32[2,256,128]{2,1,0:T(8,128)S(1)} collective-permute-done((f32[2,256,128]{2,1,0:T(8,128)S(1)}, f32[2,256,128]{2,1,0:T(8,128)S(1)}, u32[]{:S(2)}, u32[]{:S(2)}) %collective-permute-start) | collective-permute-done | bytes 262176 | tf_op jit(solution)/shard_map/ppermute | solution.py:208
  15.5 1.3 %collective-permute-start.1 = (f32[2,256,128]{2,1,0:T(8,128)S(1)}, f32[2,256,128]{2,1,0:T(8,128)S(1)}, u32[]{:S(2)}, u32[]{:S(2)}) collective-permute-start(f32[2,256,128]{2,1,0:T(8,128)S(1)} %collective-permute-done.partner), channel_id=1, source_target_pairs={{0,2},{2,4},{4,6},{3,1},{5,3},{7,5},{8,10},{10,12},{12,14},{11,9},... | collective-permute-start | bytes 786440 | tf_op jit(solution)/shard_map/ppermute | solution.py:209
  16.8 1.3 %collective-permute-start.5 = (f32[2,256,128]{2,1,0:T(8,128)S(1)}, f32[2,256,128]{2,1,0:T(8,128)S(1)}, u32[]{:S(2)}, u32[]{:S(2)}) collective-permute-start(f32[2,256,128]{2,1,0:T(8,128)S(1)} %collective-permute-done.4.partner), channel_id=1, source_target_pairs={{0,2},{2,4},{4,6},{3,1},{5,3},{7,5},{8,10},{10,12},{12,14},{11,9},... | collective-permute-start | bytes 786440 | tf_op jit(solution)/shard_map/ppermute | solution.py:209
  18.1 8.4 %collective-permute-done.1.far = f32[2,256,128]{2,1,0:T(8,128)S(1)} collective-permute-done((f32[2,256,128]{2,1,0:T(8,128)S(1)}, f32[2,256,128]{2,1,0:T(8,128)S(1)}, u32[]{:S(2)}, u32[]{:S(2)}) %collective-permute-start.1) | collective-permute-done | bytes 262176 | tf_op jit(solution)/shard_map/ppermute | solution.py:209
  26.6 1.9 %collective-permute-start.3 = (f32[3,2,128,128]{3,2,1,0:T(8,128)S(1)}, f32[3,2,128,128]{3,2,1,0:T(8,128)S(1)}, u32[]{:S(2)}, u32[]{:S(2)}) collective-permute-start(f32[3,2,128,128]{3,2,1,0:T(8,128)S(1)} %pad_maximum_fusion.2), channel_id=1, source_target_pairs={{8,0},{16,8},{24,16},{9,1},{17,9},{25,17},{10,2},{18,10},{26,18},{... | collective-permute-start | bytes 1179656 | tf_op jit(solution)/shard_map/ppermute | solution.py:211
  28.6 2.6 %collective-permute-start.2 = (f32[3,2,128,128]{3,2,1,0:T(8,128)S(1)}, f32[3,2,128,128]{3,2,1,0:T(8,128)S(1)}, u32[]{:S(2)}, u32[]{:S(2)}) collective-permute-start(f32[3,2,128,128]{3,2,1,0:T(8,128)S(1)} %pad_maximum_fusion.1), channel_id=1, source_target_pairs={{0,8},{8,16},{16,24},{1,9},{9,17},{17,25},{2,10},{10,18},{18,26},{... | collective-permute-start | bytes 1179656 | tf_op jit(solution)/shard_map/ppermute | solution.py:210
  31.2 1.9 %collective-permute-start.6 = (f32[3,2,128,128]{3,2,1,0:T(8,128)S(1)}, f32[3,2,128,128]{3,2,1,0:T(8,128)S(1)}, u32[]{:S(2)}, u32[]{:S(2)}) collective-permute-start(f32[3,2,128,128]{3,2,1,0:T(8,128)S(1)} %pad_maximum_fusion.3), channel_id=1, source_target_pairs={{0,8},{8,16},{16,24},{1,9},{9,17},{17,25},{2,10},{10,18},{18,26},{... | collective-permute-start | bytes 1179656 | tf_op jit(solution)/shard_map/ppermute | solution.py:210
  33.2 3.6 %collective-permute-start.7 = (f32[3,2,128,128]{3,2,1,0:T(8,128)S(1)}, f32[3,2,128,128]{3,2,1,0:T(8,128)S(1)}, u32[]{:S(2)}, u32[]{:S(2)}) collective-permute-start(f32[3,2,128,128]{3,2,1,0:T(8,128)S(1)} %pad_maximum_fusion.4), channel_id=1, source_target_pairs={{8,0},{16,8},{24,16},{9,1},{17,9},{25,17},{10,2},{18,10},{26,18},{... | collective-permute-start | bytes 1179656 | tf_op jit(solution)/shard_map/ppermute | solution.py:211
  36.9 0.9 collective-permute-done.2.above_ref
  37.8 7.2 %shard_map.95 = (f32[2,2,256,256]{3,2,1,0:T(8,128)S(1)}, f32[2,2,256,256]{3,2,1,0:T(8,128)S(1)}) custom-call(s32[2,3]{1,0:T(2,128)S(1)} %add_add_fusion.sc_ref, f32[2,256,256]{2,1,0:T(8,128)S(1)} %copy-done, f32[2,256,256]{2,1,0:T(8,128)S(1)} %pad_maximum_fusion.tr_ref, bf16[1536,512]{1,0:T(8,128)(2,1)} %constant.38.clone.right_ref, ...), custom_call_target="tpu_custom_call" | custom-call | flops 3221225472 | bytes 8388608 | tf_op jit(solution)/shard_map/pallas_call | solution.py:171
  45.0 1.0 %copy-done.3 = f32[2,2,256,256]{3,2,1,0:T(8,128)} copy-done((f32[2,2,256,256]{3,2,1,0:T(8,128)}, f32[2,2,256,256]{3,2,1,0:T(8,128)S(1)}, u32[]{:S(2)}) %copy-start.3) | copy-done | bytes 1048600
  46.0 7.7 %shard_map.96 = (f32[2,2,256,256]{3,2,1,0:T(8,128)S(1)}, f32[2,256,128]{2,1,0:T(8,128)S(1)}, f32[2,256,128]{2,1,0:T(8,128)S(1)}, f32[2,256,128]{2,1,0:T(8,128)S(...) custom-call(s32[2,3]{1,0:T(2,128)S(1)} %add_add_fusion.sc_ref, f32[2,2,256,256]{3,2,1,0:T(8,128)} %copy-done.3, ...), custom_call_target="tpu_custom_call" | custom-call | flops 3221225472 | bytes 8388608 | tf_op jit(solution)/shard_map/pallas_call | solution.py:171
  53.7 7.1 %shard_map.97 = (f32[2,256,128]{2,1,0:T(8,128)S(1)}, f32[2,256,128]{2,1,0:T(8,128)S(1)}, f32[2,256,128]{2,1,0:T(8,128)S(1)}, f32[3,2,128,128]{3,2,1,0:T(8,128)S(1)}, f32[3,2,128,128]{3,2,1,0:T(8,128)S(1)}) custom-call(s32[2,3]{1,0:T(2,128)S(1)} %add_add_fusion.sc_ref, f32[2,2,256,256]{3,2,1,0:T(8,128)S(1)} %get-tuple-element.16.back_ref, ...), custom_call_target="tpu_custom_call" | custom-call | flops 3221225472 | bytes 8388608 | tf_op jit(solution)/shard_map/pallas_call | solution.py:171
  60.8 1.9 %collective-permute-start.8 = (f32[3,2,128,128]{3,2,1,0:T(8,128)S(1)}, f32[3,2,128,128]{3,2,1,0:T(8,128)S(1)}, u32[]{:S(2)}, u32[]{:S(2)}) collective-permute-start(f32[3,2,128,128]{3,2,1,0:T(8,128)S(1)} %get-tuple-element.19), channel_id=1, source_target_pairs={{0,8},{8,16},{16,24},{1,9},{9,17},{17,25},{2,10},{10,18},{18,26},{... | collective-permute-start | bytes 1179656 | tf_op jit(solution)/shard_map/ppermute | solution.py:216
  62.7 3.6 %collective-permute-start.9 = (f32[3,2,128,128]{3,2,1,0:T(8,128)S(1)}, f32[3,2,128,128]{3,2,1,0:T(8,128)S(1)}, u32[]{:S(2)}, u32[]{:S(2)}) collective-permute-start(f32[3,2,128,128]{3,2,1,0:T(8,128)S(1)} %get-tuple-element.20), channel_id=1, source_target_pairs={{8,0},{16,8},{24,16},{9,1},{17,9},{25,17},{10,2},{18,10},{26,18},{... | collective-permute-start | bytes 1179656 | tf_op jit(solution)/shard_map/ppermute | solution.py:215
  66.4 1.9 %collective-permute-start.12 = (f32[3,2,128,128]{3,2,1,0:T(8,128)S(1)}, f32[3,2,128,128]{3,2,1,0:T(8,128)S(1)}, u32[]{:S(2)}, u32[]{:S(2)}) collective-permute-start(f32[3,2,128,128]{3,2,1,0:T(8,128)S(1)} %get-tuple-element.24), channel_id=1, source_target_pairs={{0,8},{8,16},{16,24},{1,9},{9,17},{17,25},{2,10},{10,18},{18,26},{... | collective-permute-start | bytes 1179656 | tf_op jit(solution)/shard_map/ppermute | solution.py:216
  68.3 3.6 %collective-permute-start.13 = (f32[3,2,128,128]{3,2,1,0:T(8,128)S(1)}, f32[3,2,128,128]{3,2,1,0:T(8,128)S(1)}, u32[]{:S(2)}, u32[]{:S(2)}) collective-permute-start(f32[3,2,128,128]{3,2,1,0:T(8,128)S(1)} %get-tuple-element.25), channel_id=1, source_target_pairs={{8,0},{16,8},{24,16},{9,1},{17,9},{25,17},{10,2},{18,10},{26,18},{... | collective-permute-start | bytes 1179656 | tf_op jit(solution)/shard_map/ppermute | solution.py:215
  72.1 3.5 %collective-permute-start.10 = (f32[2,256,128]{2,1,0:T(8,128)S(1)}, f32[2,256,128]{2,1,0:T(8,128)S(1)}, u32[]{:S(2)}, u32[]{:S(2)}) collective-permute-start(f32[2,256,128]{2,1,0:T(8,128)S(1)} %maximum_add_fusion.2), channel_id=1, source_target_pairs={{2,0},{4,2},{6,4},{1,3},{3,5},{5,7},{10,8},{12,10},{14,12},{9,11},... | collective-permute-start | bytes 786440 | tf_op jit(solution)/shard_map/ppermute | solution.py:221
  75.6 1.6 %collective-permute-done.13 = f32[3,2,128,128]{3,2,1,0:T(8,128)S(1)} collective-permute-done((f32[3,2,128,128]{3,2,1,0:T(8,128)S(1)}, f32[3,2,128,128]{3,2,1,0:T(8,128)S(1)}, u32[]{:S(2)}, u32[]{:S(2)}) %collective-permute-start.13) | collective-permute-done | bytes 393248 | tf_op jit(solution)/shard_map/ppermute | solution.py:215
  77.3 3.5 %collective-permute-start.14 = (f32[2,256,128]{2,1,0:T(8,128)S(1)}, f32[2,256,128]{2,1,0:T(8,128)S(1)}, u32[]{:S(2)}, u32[]{:S(2)}) collective-permute-start(f32[2,256,128]{2,1,0:T(8,128)S(1)} %maximum_add_fusion.5), channel_id=1, source_target_pairs={{2,0},{4,2},{6,4},{1,3},{3,5},{5,7},{10,8},{12,10},{14,12},{9,11},... | collective-permute-start | bytes 786440 | tf_op jit(solution)/shard_map/ppermute | solution.py:221
  80.8 1.5 %collective-permute-done.10 = f32[2,256,128]{2,1,0:T(8,128)S(1)} collective-permute-done((f32[2,256,128]{2,1,0:T(8,128)S(1)}, f32[2,256,128]{2,1,0:T(8,128)S(1)}, u32[]{:S(2)}, u32[]{:S(2)}) %collective-permute-start.10) | collective-permute-done | bytes 262176 | tf_op jit(solution)/shard_map/ppermute | solution.py:221
  82.3 1.0 %collective-permute-start.11 = (f32[2,256,128]{2,1,0:T(8,128)S(1)}, f32[2,256,128]{2,1,0:T(8,128)S(1)}, u32[]{:S(2)}, u32[]{:S(2)}) collective-permute-start(f32[2,256,128]{2,1,0:T(8,128)S(1)} %fusion.3), channel_id=1, source_target_pairs={{0,1},{1,0},{2,3},{3,2},{4,5},{5,4},{6,7},{7,6},{8,9},{9,8},{10,11... | collective-permute-start | bytes 786440 | tf_op jit(solution)/shard_map/ppermute | solution.py:222
  83.4 2.3 %collective-permute-done.14 = f32[2,256,128]{2,1,0:T(8,128)S(1)} collective-permute-done((f32[2,256,128]{2,1,0:T(8,128)S(1)}, f32[2,256,128]{2,1,0:T(8,128)S(1)}, u32[]{:S(2)}, u32[]{:S(2)}) %collective-permute-start.14) | collective-permute-done | bytes 262176 | tf_op jit(solution)/shard_map/ppermute | solution.py:221
  85.7 1.3 %collective-permute-start.15 = (f32[2,256,128]{2,1,0:T(8,128)S(1)}, f32[2,256,128]{2,1,0:T(8,128)S(1)}, u32[]{:S(2)}, u32[]{:S(2)}) collective-permute-start(f32[2,256,128]{2,1,0:T(8,128)S(1)} %fusion.6), channel_id=1, source_target_pairs={{0,1},{1,0},{2,3},{3,2},{4,5},{5,4},{6,7},{7,6},{8,9},{9,8},{10,11... | collective-permute-start | bytes 786440 | tf_op jit(solution)/shard_map/ppermute | solution.py:222
  87.1 4.1 %collective-permute-done.11 = f32[2,256,128]{2,1,0:T(8,128)S(1)} collective-permute-done((f32[2,256,128]{2,1,0:T(8,128)S(1)}, f32[2,256,128]{2,1,0:T(8,128)S(1)}, u32[]{:S(2)}, u32[]{:S(2)}) %collective-permute-start.11) | collective-permute-done | bytes 262176 | tf_op jit(solution)/shard_map/ppermute | solution.py:222
  91.2 3.2 %collective-permute-done.15 = f32[2,256,128]{2,1,0:T(8,128)S(1)} collective-permute-done((f32[2,256,128]{2,1,0:T(8,128)S(1)}, f32[2,256,128]{2,1,0:T(8,128)S(1)}, u32[]{:S(2)}, u32[]{:S(2)}) %collective-permute-start.15) | collective-permute-done | bytes 262176 | tf_op jit(solution)/shard_map/ppermute | solution.py:222
  94.4 1.1 %multiply_subtract_fusion = (f32[2,2,256,128]{3,2,1,0:T(8,128)}, f32[2,2,256,128]{3,2,1,0:T(8,128)}) fusion(f32[2,2,256,128]{3,2,1,0:T(8,128)S(1)} %copy-done.4, f32[1,2,256,128]{3,2,1,0:T(8,128)S(1)} %fusion.5, f32[1,2,256,128]{3,2,1,0:T(8,128)S(1)} %fusion.2, f32[2,2,256,128]{3,2,1,0:T(8,128)S(1)} %copy-done.5), kind=kLoop, calls=%fused_computation.3 | loop fusion | flops 786432 | bytes 2621440 | tf_op jit(solution)/shard_map/sub | solution.py:241
  (45 shorter events, 0.8 us)
Async XLA Ops:
  0.6 3.4 %copy-start.7 = (s32[2,2]{1,0:T(2,128)S(1)}, s32[2,2]{1,0:T(2,128)}, u32[]{:S(2)}) copy-start(s32[2,2]{1,0:T(2,128)} %param.9) | copy-start | bytes 52
  0.6 3.5 %copy-start.6 = (f32[256,256]{1,0:T(8,128)S(1)}, f32[256,256]{1,0:T(8,128)}, u32[]{:S(2)}) copy-start(f32[256,256]{1,0:T(8,128)} %param.11) | copy-start | bytes 786436
  1.8 15.0 %collective-permute-start.4 = (f32[2,256,128]{2,1,0:T(8,128)S(1)}, f32[2,256,128]{2,1,0:T(8,128)S(1)}, u32[]{:S(2)}, u32[]{:S(2)}) collective-permute-start(f32[2,256,128]{2,1,0:T(8,128)S(1)} %get-tuple-element.30.own), channel_id=1, source_target_pairs={{0,1},{1,0},{2,3},{3,2},{4,5},{5,4},{6,7},{7,6},{8,9},{9,8},{10,11... | collective-permute-start | bytes 786440 | tf_op jit(solution)/shard_map/ppermute | solution.py:208
  2.3 13.2 %collective-permute-start = (f32[2,256,128]{2,1,0:T(8,128)S(1)}, f32[2,256,128]{2,1,0:T(8,128)S(1)}, u32[]{:S(2)}, u32[]{:S(2)}) collective-permute-start(f32[2,256,128]{2,1,0:T(8,128)S(1)} %get-tuple-element.31.own), channel_id=1, source_target_pairs={{0,1},{1,0},{2,3},{3,2},{4,5},{5,4},{6,7},{7,6},{8,9},{9,8},{10,11... | collective-permute-start | bytes 786440 | tf_op jit(solution)/shard_map/ppermute | solution.py:208
  15.5 11.1 %collective-permute-start.1 = (f32[2,256,128]{2,1,0:T(8,128)S(1)}, f32[2,256,128]{2,1,0:T(8,128)S(1)}, u32[]{:S(2)}, u32[]{:S(2)}) collective-permute-start(f32[2,256,128]{2,1,0:T(8,128)S(1)} %collective-permute-done.partner), channel_id=1, source_target_pairs={{0,2},{2,4},{4,6},{3,1},{5,3},{7,5},{8,10},{10,12},{12,14},{11,9},... | collective-permute-start | bytes 786440 | tf_op jit(solution)/shard_map/ppermute | solution.py:209
  16.8 14.3 %collective-permute-start.5 = (f32[2,256,128]{2,1,0:T(8,128)S(1)}, f32[2,256,128]{2,1,0:T(8,128)S(1)}, u32[]{:S(2)}, u32[]{:S(2)}) collective-permute-start(f32[2,256,128]{2,1,0:T(8,128)S(1)} %collective-permute-done.4.partner), channel_id=1, source_target_pairs={{0,2},{2,4},{4,6},{3,1},{5,3},{7,5},{8,10},{10,12},{12,14},{11,9},... | collective-permute-start | bytes 786440 | tf_op jit(solution)/shard_map/ppermute | solution.py:209
  26.6 10.3 %collective-permute-start.3 = (f32[3,2,128,128]{3,2,1,0:T(8,128)S(1)}, f32[3,2,128,128]{3,2,1,0:T(8,128)S(1)}, u32[]{:S(2)}, u32[]{:S(2)}) collective-permute-start(f32[3,2,128,128]{3,2,1,0:T(8,128)S(1)} %pad_maximum_fusion.2), channel_id=1, source_target_pairs={{8,0},{16,8},{24,16},{9,1},{17,9},{25,17},{10,2},{18,10},{26,18},{... | collective-permute-start | bytes 1179656 | tf_op jit(solution)/shard_map/ppermute | solution.py:211
  28.6 9.3 %copy-start = (f32[2,256,256]{2,1,0:T(8,128)S(1)}, f32[2,256,256]{2,1,0:T(8,128)}, u32[]{:S(2)}) copy-start(f32[2,256,256]{2,1,0:T(8,128)} %probe_ref.1) | copy-start | bytes 1572868
  28.6 9.2 %copy-start.2 = (bf16[512,768]{1,0:T(8,128)(2,1)S(1)}, bf16[512,768]{1,0:T(8,128)(2,1)}, u32[]{:S(2)}) copy-start(bf16[512,768]{1,0:T(8,128)(2,1)} %constant.39.clone.left_ref) | copy-start | bytes 2359300
  28.6 9.2 %collective-permute-start.2 = (f32[3,2,128,128]{3,2,1,0:T(8,128)S(1)}, f32[3,2,128,128]{3,2,1,0:T(8,128)S(1)}, u32[]{:S(2)}, u32[]{:S(2)}) collective-permute-start(f32[3,2,128,128]{3,2,1,0:T(8,128)S(1)} %pad_maximum_fusion.1), channel_id=1, source_target_pairs={{0,8},{8,16},{16,24},{1,9},{9,17},{17,25},{2,10},{10,18},{18,26},{... | collective-permute-start | bytes 1179656 | tf_op jit(solution)/shard_map/ppermute | solution.py:210
  31.2 14.8 %collective-permute-start.6 = (f32[3,2,128,128]{3,2,1,0:T(8,128)S(1)}, f32[3,2,128,128]{3,2,1,0:T(8,128)S(1)}, u32[]{:S(2)}, u32[]{:S(2)}) collective-permute-start(f32[3,2,128,128]{3,2,1,0:T(8,128)S(1)} %pad_maximum_fusion.3), channel_id=1, source_target_pairs={{0,8},{8,16},{16,24},{1,9},{9,17},{17,25},{2,10},{10,18},{18,26},{... | collective-permute-start | bytes 1179656 | tf_op jit(solution)/shard_map/ppermute | solution.py:210
  33.2 12.8 %collective-permute-start.7 = (f32[3,2,128,128]{3,2,1,0:T(8,128)S(1)}, f32[3,2,128,128]{3,2,1,0:T(8,128)S(1)}, u32[]{:S(2)}, u32[]{:S(2)}) collective-permute-start(f32[3,2,128,128]{3,2,1,0:T(8,128)S(1)} %pad_maximum_fusion.4), channel_id=1, source_target_pairs={{8,0},{16,8},{24,16},{9,1},{17,9},{25,17},{10,2},{18,10},{26,18},{... | collective-permute-start | bytes 1179656 | tf_op jit(solution)/shard_map/ppermute | solution.py:211
  36.9 9.1 %copy-start.1 = (f32[2,256,256]{2,1,0:T(8,128)S(1)}, f32[2,256,256]{2,1,0:T(8,128)}, u32[]{:S(2)}) copy-start(f32[2,256,256]{2,1,0:T(8,128)} %intensity_ref.1) | copy-start | bytes 1572868
  45.0 1.0 %copy-start.3 = (f32[2,2,256,256]{3,2,1,0:T(8,128)}, f32[2,2,256,256]{3,2,1,0:T(8,128)S(1)}, u32[]{:S(2)}) copy-start(f32[2,2,256,256]{3,2,1,0:T(8,128)S(1)} %get-tuple-element.15.phi_ref) | copy-start | bytes 3145732
  60.8 11.2 %collective-permute-start.8 = (f32[3,2,128,128]{3,2,1,0:T(8,128)S(1)}, f32[3,2,128,128]{3,2,1,0:T(8,128)S(1)}, u32[]{:S(2)}, u32[]{:S(2)}) collective-permute-start(f32[3,2,128,128]{3,2,1,0:T(8,128)S(1)} %get-tuple-element.19), channel_id=1, source_target_pairs={{0,8},{8,16},{16,24},{1,9},{9,17},{17,25},{2,10},{10,18},{18,26},{... | collective-permute-start | bytes 1179656 | tf_op jit(solution)/shard_map/ppermute | solution.py:216
  62.7 9.3 %collective-permute-start.9 = (f32[3,2,128,128]{3,2,1,0:T(8,128)S(1)}, f32[3,2,128,128]{3,2,1,0:T(8,128)S(1)}, u32[]{:S(2)}, u32[]{:S(2)}) collective-permute-start(f32[3,2,128,128]{3,2,1,0:T(8,128)S(1)} %get-tuple-element.20), channel_id=1, source_target_pairs={{8,0},{16,8},{24,16},{9,1},{17,9},{25,17},{10,2},{18,10},{26,18},{... | collective-permute-start | bytes 1179656 | tf_op jit(solution)/shard_map/ppermute | solution.py:215
  66.4 9.2 %collective-permute-start.12 = (f32[3,2,128,128]{3,2,1,0:T(8,128)S(1)}, f32[3,2,128,128]{3,2,1,0:T(8,128)S(1)}, u32[]{:S(2)}, u32[]{:S(2)}) collective-permute-start(f32[3,2,128,128]{3,2,1,0:T(8,128)S(1)} %get-tuple-element.24), channel_id=1, source_target_pairs={{0,8},{8,16},{16,24},{1,9},{9,17},{17,25},{2,10},{10,18},{18,26},{... | collective-permute-start | bytes 1179656 | tf_op jit(solution)/shard_map/ppermute | solution.py:216
  68.3 8.9 %collective-permute-start.13 = (f32[3,2,128,128]{3,2,1,0:T(8,128)S(1)}, f32[3,2,128,128]{3,2,1,0:T(8,128)S(1)}, u32[]{:S(2)}, u32[]{:S(2)}) collective-permute-start(f32[3,2,128,128]{3,2,1,0:T(8,128)S(1)} %get-tuple-element.25), channel_id=1, source_target_pairs={{8,0},{16,8},{24,16},{9,1},{17,9},{25,17},{10,2},{18,10},{26,18},{... | collective-permute-start | bytes 1179656 | tf_op jit(solution)/shard_map/ppermute | solution.py:215
  72.1 10.2 %collective-permute-start.10 = (f32[2,256,128]{2,1,0:T(8,128)S(1)}, f32[2,256,128]{2,1,0:T(8,128)S(1)}, u32[]{:S(2)}, u32[]{:S(2)}) collective-permute-start(f32[2,256,128]{2,1,0:T(8,128)S(1)} %maximum_add_fusion.2), channel_id=1, source_target_pairs={{2,0},{4,2},{6,4},{1,3},{3,5},{5,7},{10,8},{12,10},{14,12},{9,11},... | collective-permute-start | bytes 786440 | tf_op jit(solution)/shard_map/ppermute | solution.py:221
  77.3 8.4 %collective-permute-start.14 = (f32[2,256,128]{2,1,0:T(8,128)S(1)}, f32[2,256,128]{2,1,0:T(8,128)S(1)}, u32[]{:S(2)}, u32[]{:S(2)}) collective-permute-start(f32[2,256,128]{2,1,0:T(8,128)S(1)} %maximum_add_fusion.5), channel_id=1, source_target_pairs={{2,0},{4,2},{6,4},{1,3},{3,5},{5,7},{10,8},{12,10},{14,12},{9,11},... | collective-permute-start | bytes 786440 | tf_op jit(solution)/shard_map/ppermute | solution.py:221
  82.3 8.8 %collective-permute-start.11 = (f32[2,256,128]{2,1,0:T(8,128)S(1)}, f32[2,256,128]{2,1,0:T(8,128)S(1)}, u32[]{:S(2)}, u32[]{:S(2)}) collective-permute-start(f32[2,256,128]{2,1,0:T(8,128)S(1)} %fusion.3), channel_id=1, source_target_pairs={{0,1},{1,0},{2,3},{3,2},{4,5},{5,4},{6,7},{7,6},{8,9},{9,8},{10,11... | collective-permute-start | bytes 786440 | tf_op jit(solution)/shard_map/ppermute | solution.py:222
  85.7 8.7 %copy-start.4 = (f32[2,2,256,128]{3,2,1,0:T(8,128)S(1)}, f32[2,2,256,128]{3,2,1,0:T(8,128)}, u32[]{:S(2)}) copy-start(f32[2,2,256,128]{3,2,1,0:T(8,128)} %param.12) | copy-start | bytes 1572868
  85.7 8.7 %copy-start.5 = (f32[2,2,256,128]{3,2,1,0:T(8,128)S(1)}, f32[2,2,256,128]{3,2,1,0:T(8,128)}, u32[]{:S(2)}) copy-start(f32[2,2,256,128]{3,2,1,0:T(8,128)} %param.13) | copy-start | bytes 1572868
  85.7 8.6 %collective-permute-start.15 = (f32[2,256,128]{2,1,0:T(8,128)S(1)}, f32[2,256,128]{2,1,0:T(8,128)S(1)}, u32[]{:S(2)}, u32[]{:S(2)}) collective-permute-start(f32[2,256,128]{2,1,0:T(8,128)S(1)} %fusion.6), channel_id=1, source_target_pairs={{0,1},{1,0},{2,3},{3,2},{4,5},{5,4},{6,7},{7,6},{8,9},{9,8},{10,11... | collective-permute-start | bytes 786440 | tf_op jit(solution)/shard_map/ppermute | solution.py:222
where the time goes:
time: 97 us; the launch traced here: 95.5 us
  starting transfers between devices  35.2 us (36%)
  waiting for transfers between devices  32.4 us (33%)
  Pallas kernels  22 us (23%)
  local copies, waits for them, and re-layouts  3.35 us (3%)
  other arithmetic  1.65 us (2%)
  between operations  1.01 us (1%)
    pallas_call x3, Pallas kernels, call(): pl.pallas_call(kernel, out_shape=[jax.ShapeDtypeStruct(s, jnp.float32) fo...  22 us
    ppermute x2, waiting for transfers between devices, halo(): partner = lax.ppermute(own, 'tx', swap)  10.4 us
    ppermute x2, waiting for transfers between devices, halo(): far = lax.ppermute(partner, 'tx', relay)  8.41 us
    ppermute x2, starting transfers between devices, fold(): from_below = lax.ppermute(above, 'ty', up)  7.28 us
    ppermute x2, waiting for transfers between devices, fold(): partner_in = lax.ppermute(rows(partner, 1) + far_in, 'tx', swap)  7.25 us
    ppermute x2, starting transfers between devices, fold(): far_in = lax.ppermute(rows(far, 2), 'tx', back)  6.99 us
    ppermute x2, starting transfers between devices, halo(): lax.ppermute(jnp.stack([t[:, :h] for t in (own, partner, far)]), 'ty', up)  5.56 us
    ppermute x2, starting transfers between devices, halo(): lax.ppermute(jnp.stack([t[:, h:] for t in (own, partner, far)]), 'ty', down)  4.48 us
  transfers between devices with their start and end apart: 16, of which 8 were waited for; matrix products, arithmetic and copies ran while one was open for 2% of the time, Pallas kernels for 8%

commit v1 on v0

v1 whole, which is shorter than its diff:
```python
import functools
import math

import jax
import jax.numpy as jnp
import numpy as np
from jax import lax
from jax.experimental import pallas as pl
from jax.experimental.pallas import tpu as pltpu
from jax.sharding import PartitionSpec as P

decay_rate = 0.9
grad_scale = 0.05
step_length = 0.5

VMEM = pl.BlockSpec(memory_space=pltpu.VMEM)
ANY = pl.BlockSpec(memory_space=pl.ANY)
SMEM = pl.BlockSpec(memory_space=pltpu.SMEM)


def dft_tables(n):
    k = np.arange(n)
    angle = 2.0 * math.pi * (np.outer(k, k) % n) / n
    c, s = np.cos(angle) / math.sqrt(n), -np.sin(angle) / math.sqrt(n)
    right = np.block([[c, s], [-s, c]]).astype(np.float32)
    left = np.concatenate([c, s], axis=0).astype(np.float32)

    def split(t):
        hi = t.astype(jnp.bfloat16)
        lo = (t - hi.astype(np.float32)).astype(jnp.bfloat16)
        return hi, lo

    rh, rl = split(right)
    lh, ll = split(left)
    return (
        jnp.asarray(np.concatenate([rh, rh, rl], axis=0)),
        jnp.asarray(np.concatenate([lh, lh, ll], axis=1)),
    )


def halves(x):
    hi = x.astype(jnp.bfloat16)
    lo = (x - hi.astype(jnp.float32)).astype(jnp.bfloat16)
    return hi, lo


def fft2(xr, xi, right_ref, left_ref):
    n = xr.shape[-1]
    hi, lo = halves(jnp.concatenate([xr, xi], axis=1))
    y = jnp.dot(
        jnp.concatenate([hi, lo, hi], axis=1), right_ref[...], preferred_element_type=jnp.float32
    )
    hi, lo = halves(y)
    z = jnp.dot(
        left_ref[...], jnp.concatenate([hi, lo, hi], axis=0), preferred_element_type=jnp.float32
    )
    return z[:n, :n] - z[n:, n:], z[:n, n:] + z[n:, :n]


def ifft2(xr, xi, right_ref, left_ref):
    yi, yr = fft2(xi, xr, right_ref, left_ref)
    return yr, yi


def mul(ar, ai, br, bi):
    return ar * br - ai * bi, ar * bi + ai * br


def masks(sc_ref, p, n, odd):
    r, c = sc_ref[p, 0], sc_ref[p, 1]
    h = n // 2
    rows = lax.broadcasted_iota(jnp.int32, (n, h), 0)
    cols = lax.broadcasted_iota(jnp.int32, (n, h), 1)
    later = (cols >= c).astype(jnp.int32)
    return rows >= r, (later + odd) == 1


def window(q, tiles, edge, mask, n):
    h = n // 2
    row_first, use_far = mask
    cols = []
    for t, tile in enumerate(tiles):
        top = jnp.where(row_first[:h], edge[1, t, q], tile[q, h:, :])
        bottom = jnp.where(row_first[h:], tile[q, :h, :], edge[0, t, q])
        cols.append(jnp.concatenate([top, bottom], axis=0))
    own, partner, far = cols
    return jnp.concatenate([jnp.where(use_far, far, partner), own], axis=1)


def scatter(g, q, g_tile, g_edge, mask, n):
    h = n // 2
    row_first, use_far = mask
    left, own = g[:, :h], g[:, h:]
    zero = jnp.zeros_like(left)
    parts = (own, jnp.where(use_far, zero, left), jnp.where(use_far, left, zero))
    for t, v in enumerate(parts):
        low = jnp.where(row_first, v, zero)
        high = jnp.where(row_first, zero, v)
        g_edge[1, t, q] += low[:h]
        g_tile[t, q, h:, :] += high[:h]
        g_tile[t, q, :h, :] += low[h:]
        g_edge[0, t, q] += high[h:]


def kernel(
    sizes, sc_ref, own, probe_ref, phase_ref, intensity_hbm, right_hbm, left_hbm, out_ref,
    right_ref, left_ref, intensity_ref, tr_ref, roll_ref, phi_ref, back_ref,
    part, far, edge, g_tile, g_edge, rows_in, far_in, part_in,
    local_sem, m_send, m_recv, f_send, f_recv, e_send, e_recv,
    r_send, r_recv, gf_send, gf_recv, gp_send, gp_recv,
):
    nty, ntx = sizes
    count, n = intensity_ref.shape[0], intensity_ref.shape[-1]
    h = n // 2
    iy, ix = lax.axis_index("ty"), lax.axis_index("tx")
    odd = lax.rem(ix, 2)
    partner = ix + 1 - 2 * odd
    target = ix + 2 - 4 * odd
    source = ix - 2 + 4 * odd
    has_target = jnp.logical_and(target >= 0, target < ntx)
    has_source = jnp.logical_and(source >= 0, source < ntx)
    has_up, has_down = iy > 0, iy < nty - 1
    vertical = ((iy - 1, has_up), (iy + 1, has_down))

    loads = [
        pltpu.make_async_copy(a, b, local_sem.at[i])
        for i, (a, b) in enumerate(
            ((right_hbm, right_ref), (left_hbm, left_ref), (intensity_hbm, intensity_ref))
        )
    ]
    for load in loads:
        load.start()

    barrier = pltpu.get_barrier_semaphore()

    def greet(dev):
        pl.semaphore_signal(barrier, inc=1, device_id=dev, device_id_type=pl.DeviceIdType.MESH)

    greet((iy, partner))
    for cond, dev in (
        (has_target, (iy, target)),
        (has_source, (iy, source)),
        (has_up, (iy - 1, ix)),
        (has_down, (iy + 1, ix)),
    ):
        pl.when(cond)(functools.partial(greet, dev))
    peers = 1 + sum(cond.astype(jnp.int32) for cond in (has_target, has_source, has_up, has_down))
    pl.semaphore_wait(barrier, peers)

    def remote(src, dst, send, recv, dev):
        return pltpu.make_async_remote_copy(
            src_ref=src, dst_ref=dst, send_sem=send, recv_sem=recv,
            device_id=dev, device_id_type=pl.DeviceIdType.MESH,
        )

    def half(b):
        return pl.ds(b * h, h)

    def swap_copy(s, q, b):
        return remote(own.at[s, q, half(b)], part.at[s, q, half(b)], m_send.at[s, q, b], m_recv.at[s, q, b], (iy, partner))

    def relay_copy(s, q, b):
        return remote(part.at[s, q, half(b)], far.at[s, q, half(b)], f_send.at[s, q, b], f_recv.at[s, q, b], (iy, target))

    def edge_copy(s, q, b, t):
        src = (own, part, far)[t]
        return remote(src.at[s, q, half(b)], edge.at[s, b, t, q], e_send.at[s, b, t, q], e_recv.at[s, b, t, q], (vertical[b][0], ix))

    def rows_copy(s, q, b, t):
        return remote(g_edge.at[s, b, t, q], rows_in.at[s, b, t, q], r_send.at[s, b, t, q], r_recv.at[s, b, t, q], (vertical[1 - b][0], ix))

    def far_copy(s, q, b):
        return remote(g_tile.at[s, 2, q, half(b)], far_in.at[s, q, half(b)], gf_send.at[s, q, b], gf_recv.at[s, q, b], (iy, source))

    def part_copy(s, q, b):
        return remote(g_tile.at[s, 1, q, half(b)], part_in.at[s, q, half(b)], gp_send.at[s, q, b], gp_recv.at[s, q, b], (iy, partner))

    chunks = [(q, b) for q in (0, 1) for b in (0, 1)]

    def start_own(s):
        for q, b in chunks:
            swap_copy(s, q, b).start()

    def start_own_edges(s):
        for q, b in chunks:
            pl.when(vertical[b][1])(lambda q=q, b=b: edge_copy(s, q, b, 0).start())

    def on_swap(s):
        for q, b in chunks:
            swap_copy(s, q, b).wait_recv()
            pl.when(has_target)(lambda q=q, b=b: relay_copy(s, q, b).start())
            pl.when(vertical[b][1])(lambda q=q, b=b: edge_copy(s, q, b, 1).start())

    def on_relay(s):
        @pl.when(has_source)
        def _():
            for q, b in chunks:
                relay_copy(s, q, b).wait_recv()
                pl.when(vertical[b][1])(lambda q=q, b=b: edge_copy(s, q, b, 2).start())

    def on_edges(s):
        for q, b in chunks:
            @pl.when(vertical[1 - b][1])
            def _(q=q, b=b):
                edge_copy(s, q, b, 0).wait_recv()
                edge_copy(s, q, b, 1).wait_recv()
                pl.when(has_source)(lambda: edge_copy(s, q, b, 2).wait_recv())

    def send_rows(s):
        for t in (2, 1, 0):
            for q, b in chunks:
                pl.when(vertical[1 - b][1])(lambda q=q, b=b, t=t: rows_copy(s, q, b, t).start())

    def add_rows(s, q, b, t):
        @pl.when(vertical[b][1])
        def _():
            rows_copy(s, q, b, t).wait_recv()
            g_tile[s, t, q, half(b), :] += rows_in[s, b, t, q]

    def send_far(s):
        @pl.when(has_source)
        def _():
            for q, b in chunks:
                add_rows(s, q, b, 2)
                far_copy(s, q, b).start()

        @pl.when(jnp.logical_not(has_source))
        def _():
            for q, b in chunks:
                add_rows(s, q, b, 2)

    def send_part(s):
        for q, b in chunks:
            add_rows(s, q, b, 1)

            @pl.when(has_target)
            def _(q=q, b=b):
                far_copy(s, q, b).wait_recv()
                g_tile[s, 1, q, half(b), :] += far_in[s, q, half(b), :]

            part_copy(s, q, b).start()

    def finish(s):
        for q, b in chunks:
            add_rows(s, q, b, 0)
            part_copy(s, q, b).wait_recv()
            out_ref[s, q, half(b), :] = g_tile[s, 0, q, half(b), :] + part_in[s, q, half(b), :]

    start_own(0)
    start_own_edges(0)
    start_own(1)
    start_own_edges(1)
    tr_ref[0] = jnp.cos(phase_ref[...])
    tr_ref[1] = jnp.sin(phase_ref[...])
    for p in range(count):
        r, c = lax.rem(sc_ref[p, 0], n), sc_ref[p, 1]
        roll_ref[p, 0] = pltpu.roll(pltpu.roll(probe_ref[0], c, 1), r, 0)
        roll_ref[p, 1] = pltpu.roll(pltpu.roll(probe_ref[1], c, 1), r, 0)
    g_tile[...] = jnp.zeros_like(g_tile)
    g_edge[...] = jnp.zeros_like(g_edge)
    for load in loads:
        load.wait()
    on_swap(0)
    on_relay(0)
    on_swap(1)
    on_edges(0)

    def first(p, carry):
        @pl.when(p == 1)
        def _():
            on_relay(1)

        mask = masks(sc_ref, p, n, odd)
        tiles = (own.at[0], part.at[0], far.at[0])
        wr = window(0, tiles, edge.at[0], mask, n)
        wi = window(1, tiles, edge.at[0], mask, n)
        xr, xi = fft2(*mul(roll_ref[p, 0], roll_ref[p, 1], wr, wi), right_ref, left_ref)
        xr, xi = ifft2(*mul(tr_ref[0], tr_ref[1], xr, xi), right_ref, left_ref)
        phi_ref[p, 0] = xr
        phi_ref[p, 1] = xi
        return carry

    lax.fori_loop(0, count, first, 0)
    if count == 1:
        on_relay(1)
    on_edges(1)

    def second(p, carry):
        mask = masks(sc_ref, p, n, odd)
        tiles = (own.at[1], part.at[1], far.at[1])
        wr = window(0, tiles, edge.at[1], mask, n)
        wi = window(1, tiles, edge.at[1], mask, n)
        fr, fi = fft2(*mul(phi_ref[p, 0], phi_ref[p, 1], wr, wi), right_ref, left_ref)
        res = 2.0 * (fr * fr + fi * fi - intensity_ref[p])
        br, bi = ifft2(res * fr, res * fi, right_ref, left_ref)
        zr, zi = mul(wr, -wi, br, bi)
        back_ref[p, 0] = zr
        back_ref[p, 1] = zi
        gr, gi = mul(phi_ref[p, 0], -phi_ref[p, 1], br, bi)
        scatter(gr, 0, g_tile.at[1], g_edge.at[1], mask, n)
        scatter(gi, 1, g_tile.at[1], g_edge.at[1], mask, n)
        return carry

    lax.fori_loop(0, count, second, 0)
    send_rows(1)

    def third(p, carry):
        mask = masks(sc_ref, p, n, odd)
        xr, xi = fft2(back_ref[p, 0], back_ref[p, 1], right_ref, left_ref)
        xr, xi = mul(tr_ref[0], -tr_ref[1], xr, xi)
        back_ref[p, 0] = xr
        back_ref[p, 1] = xi

        @pl.when(p == 0)
        def _():
            send_far(1)

        @pl.when(p == 1)
        def _():
            send_part(1)

        xr, xi = ifft2(back_ref[p, 0], back_ref[p, 1], right_ref, left_ref)
        gr, gi = mul(roll_ref[p, 0], -roll_ref[p, 1], xr, xi)
        scatter(gr, 0, g_tile.at[0], g_edge.at[0], mask, n)
        scatter(gi, 1, g_tile.at[0], g_edge.at[0], mask, n)
        return carry

    lax.fori_loop(0, count, third, 0)
    if count == 1:
        send_part(1)
    send_rows(0)
    send_far(0)
    send_part(0)
    finish(1)
    finish(0)
    for s in (0, 1):
        for q, b in chunks:
            swap_copy(s, q, b).wait_send()
            part_copy(s, q, b).wait_send()
            pl.when(has_target)(lambda s=s, q=q, b=b: relay_copy(s, q, b).wait_send())
            pl.when(has_source)(lambda s=s, q=q, b=b: far_copy(s, q, b).wait_send())

            @pl.when(vertical[b][1])
            def _(s=s, q=q, b=b):
                edge_copy(s, q, b, 0).wait_send()
                edge_copy(s, q, b, 1).wait_send()
                pl.when(has_source)(lambda: edge_copy(s, q, b, 2).wait_send())

            @pl.when(vertical[1 - b][1])
            def _(s=s, q=q, b=b):
                for t in (0, 1, 2):
                    rows_copy(s, q, b, t).wait_send()


def on_device(intensity, corner, probe, prop_phase, object_slices, momentum):
    count, n = intensity.shape[0], intensity.shape[-1]
    h = n // 2
    _, _, tile_rows, tile_cols = object_slices.shape
    assert tile_rows == n and tile_cols == h
    nty, ntx = lax.axis_size("ty"), lax.axis_size("tx")
    assert ntx % 2 == 0
    iy, ix = lax.axis_index("ty"), lax.axis_index("tx")
    sc = jnp.stack([corner[:, 0] - (iy * tile_rows - h), corner[:, 1] - (ix * tile_cols - h)], axis=1)
    right, left = dft_tables(n)
    f32 = jnp.float32
    field = pltpu.VMEM((count, 2, n, n), f32)
    dma = pltpu.SemaphoreType.DMA
    tiles, edges = (2, 2, n, h), (2, 2, 3, 2, h, h)
    gradient = pl.pallas_call(
        functools.partial(kernel, (nty, ntx)),
        out_shape=jax.ShapeDtypeStruct(object_slices.shape, f32),
        in_specs=[SMEM, VMEM, VMEM, VMEM, ANY, ANY, ANY],
        out_specs=VMEM,
        scratch_shapes=[
            pltpu.VMEM(right.shape, right.dtype),
            pltpu.VMEM(left.shape, left.dtype),
            pltpu.VMEM(intensity.shape, f32),
            pltpu.VMEM((2, n, n), f32),
            field,
            field,
            field,
            pltpu.VMEM(tiles, f32),
            pltpu.VMEM(tiles, f32),
            pltpu.VMEM(edges, f32),
            pltpu.VMEM((2, 3, 2, n, h), f32),
            pltpu.VMEM(edges, f32),
            pltpu.VMEM(edges, f32),
            pltpu.VMEM(tiles, f32),
            pltpu.VMEM(tiles, f32),
            dma((3,)),
        ]
        + [dma((2, 2, 2))] * 4
        + [dma((2, 2, 3, 2))] * 4
        + [dma((2, 2, 2))] * 4,
        compiler_params=pltpu.CompilerParams(
            collective_id=0, has_side_effects=True, vmem_limit_bytes=48 << 20
        ),
    )(sc, object_slices, probe, prop_phase, intensity, right, left)
    momentum_next = decay_rate * momentum + grad_scale * gradient
    object_next = object_slices - step_length * momentum_next
    return (object_next, momentum_next)


def solution(mesh):
    return jax.shard_map(
        on_device,
        mesh=mesh,
        in_specs=(
            P(("ty", "tx"), None, None),
            P(("ty", "tx"), None),
            P(),
            P(),
            P(None, None, "ty", "tx"),
            P(None, None, "ty", "tx"),
        ),
        out_specs=(P(None, None, "ty", "tx"), P(None, None, "ty", "tx")),
        check_vma=False,
    )
```

time: 97 us -> 62.1 us (0.64); the launches traced: 95.5 us -> 61.7 us
  starting transfers between devices: 35.2 us -> 0 us
  waiting for transfers between devices: 32.4 us -> 0 us
  Pallas kernels: 22 us -> 52.4 us
  local copies, waits for them, and re-layouts: 3.35 us -> 6.62 us
    ppermute x16 -> x0, starting transfers between devices: 35.2 us -> none  [the longest x2 7.28 us: fold(): from_below = lax.ppermute(above, 'ty', up)]
    ppermute x16 -> x0, waiting for transfers between devices: 32.4 us -> none  [the longest x2 10.4 us: halo(): partner = lax.ppermute(own, 'tx', swap)]
    pallas_call x3 -> x1, Pallas kernels: 22 us -> 52.4 us  [on_device(): pl.pallas_call(functools.partial(kernel, (nty, ntx)), out_shape=jax.Shape...]
    unnamed x16 -> x14, local copies, waits for them, and re-layouts: 1 us -> 6.62 us
    squeeze x5 -> x0, local copies, waits for them, and re-layouts: 1.22 us -> none  [the longest x1 1.11 us: halo(): own = object_slices[s]]
    another operation x7 -> x0, local copies, waits for them, and re-layouts: 1.13 us -> none  [the longest x1 0.95 us: on_device(): transfer = jnp.stack([jnp.cos(prop_phase), jnp.sin(prop_phase)])]
  transfers between devices with their start and end apart: 16 -> 0, of which waited for: 8 -> 0; matrix products, arithmetic and copies ran while one was open for 2% -> 0% of each run, Pallas kernels for 8% -> 0%
where the time goes in v1:
time: 62.1 us; the launch traced here: 61.7 us
  Pallas kernels  52.4 us (84%)
  local copies, waits for them, and re-layouts  6.62 us (11%)
  other arithmetic  1.99 us (3%)
  between operations  0.66 us (1%)
    pallas_call x1, Pallas kernels, on_device(): pl.pallas_call(functools.partial(kernel, (nty, ntx)), out_shape=jax.Shape...  52.4 us
    unnamed x14, local copies, waits for them, and re-layouts  6.62 us

profile of v1, /device:TPU:6, one launch (start us, length us, event | category | flops | bytes accessed | tf_op | source)
XLA Modules:
  0.0 61.7 jit_solution(15167110098008970691)
XLA Ops:
  0.6 0.8 %slice_subtract_fusion.1 = (s32[2,1]{1,0:T(2,128)S(1)}, s32[2,1]{1,0:T(2,128)S(1)}) fusion(s32[2,2]{1,0:T(2,128)} %param.9, s32[]{:T(128)S(6)} %sub.23, s32[]{:T(128)S(6)} %sub.26), kind=kLoop, calls=%fused_computation.4 | loop fusion | flops 4 | bytes 40 | tf_op jit(solution)/shard_map/sub | solution.py:363
  1.5 0.1 pad_add_fusion.sc_ref
  1.5 0.0 copy-start
  1.5 1.0 %copy-done = f32[2,2,256,128]{3,2,1,0:T(8,128)S(1)} copy-done((f32[2,2,256,128]{3,2,1,0:T(8,128)S(1)}, f32[2,2,256,128]{3,2,1,0:T(8,128)}, u32[]{:S(2)}) %copy-start) | copy-done | bytes 524312
  2.6 0.0 copy-start.1
  2.6 1.4 %copy-done.1 = bf16[1536,512]{1,0:T(8,128)(2,1)S(1)} copy-done((bf16[1536,512]{1,0:T(8,128)(2,1)S(1)}, bf16[1536,512]{1,0:T(8,128)(2,1)}, u32[]{:S(2)}) %copy-start.1) | copy-done | bytes 1572888
  4.0 0.0 copy-start.2
  4.0 1.1 %copy-done.2 = bf16[512,768]{1,0:T(8,128)(2,1)S(1)} copy-done((bf16[512,768]{1,0:T(8,128)(2,1)S(1)}, bf16[512,768]{1,0:T(8,128)(2,1)}, u32[]{:S(2)}) %copy-start.2) | copy-done | bytes 786456
  5.1 0.0 copy-start.3
  5.1 1.0 %copy-done.3 = f32[2,256,256]{2,1,0:T(8,128)S(1)} copy-done((f32[2,256,256]{2,1,0:T(8,128)S(1)}, f32[2,256,256]{2,1,0:T(8,128)}, u32[]{:S(2)}) %copy-start.3) | copy-done | bytes 524312
  6.2 0.0 copy-start.4
  6.2 1.0 %copy-done.4 = f32[2,256,256]{2,1,0:T(8,128)S(1)} copy-done((f32[2,256,256]{2,1,0:T(8,128)S(1)}, f32[2,256,256]{2,1,0:T(8,128)}, u32[]{:S(2)}) %copy-start.4) | copy-done | bytes 524312
  7.2 0.0 copy-start.5
  7.2 0.9 %copy-done.5 = f32[256,256]{1,0:T(8,128)S(1)} copy-done((f32[256,256]{1,0:T(8,128)S(1)}, f32[256,256]{1,0:T(8,128)}, u32[]{:S(2)}) %copy-start.5) | copy-done | bytes 262168
  8.2 0.0 copy-start.6
  8.2 52.4 %shard_map.95 = f32[2,2,256,128]{3,2,1,0:T(8,128)S(1)} custom-call(s32[2,2]{1,0:T(2,128)S(1)} %pad_add_fusion.sc_ref, f32[2,2,256,128]{3,2,1,0:T(8,128)S(1)} %copy-done, f32[2,256,256]{2,1,0:T(8,128)S(1)} %copy-done.3, f32[256,256]{1,0:T(8,128)S(1)} %copy-done.5, f32[2,256,256]{2,1,0:T(8,128)S(1)} %copy-done.4, bf16[1536,512]{1,0:T(8,128)(2,1)S(1)} %copy-done.1, ...), custom_call_target="tpu_custom_call" | custom-call | tf_op jit(solution)/shard_map/pallas_call | solution.py:369
  60.6 0.0 copy-done.6
  60.6 1.1 %multiply_subtract_fusion = (f32[2,2,256,128]{3,2,1,0:T(8,128)}, f32[2,2,256,128]{3,2,1,0:T(8,128)}) fusion(f32[2,2,256,128]{3,2,1,0:T(8,128)S(1)} %copy-done, f32[2,2,256,128]{3,2,1,0:T(8,128)S(1)} %shard_map.95, f32[2,2,256,128]{3,2,1,0:T(8,128)S(1)} %copy-done.6), kind=kLoop, calls=%fused_computation | loop fusion | flops 655360 | bytes 2621440 | tf_op jit(solution)/shard_map/sub | solution.py:400
Async XLA Ops:
  1.5 1.0 %copy-start = (f32[2,2,256,128]{3,2,1,0:T(8,128)S(1)}, f32[2,2,256,128]{3,2,1,0:T(8,128)}, u32[]{:S(2)}) copy-start(f32[2,2,256,128]{3,2,1,0:T(8,128)} %own.1) | copy-start | bytes 1572868
  2.6 1.4 %copy-start.1 = (bf16[1536,512]{1,0:T(8,128)(2,1)S(1)}, bf16[1536,512]{1,0:T(8,128)(2,1)}, u32[]{:S(2)}) copy-start(bf16[1536,512]{1,0:T(8,128)(2,1)} %constant.25.clone.right_hbm) | copy-start | bytes 4718596
  4.0 1.1 %copy-start.2 = (bf16[512,768]{1,0:T(8,128)(2,1)S(1)}, bf16[512,768]{1,0:T(8,128)(2,1)}, u32[]{:S(2)}) copy-start(bf16[512,768]{1,0:T(8,128)(2,1)} %constant.26.clone.left_hbm) | copy-start | bytes 2359300
  5.1 1.0 %copy-start.3 = (f32[2,256,256]{2,1,0:T(8,128)S(1)}, f32[2,256,256]{2,1,0:T(8,128)}, u32[]{:S(2)}) copy-start(f32[2,256,256]{2,1,0:T(8,128)} %probe_ref.1) | copy-start | bytes 1572868
  6.2 1.0 %copy-start.4 = (f32[2,256,256]{2,1,0:T(8,128)S(1)}, f32[2,256,256]{2,1,0:T(8,128)}, u32[]{:S(2)}) copy-start(f32[2,256,256]{2,1,0:T(8,128)} %intensity_hbm.1) | copy-start | bytes 1572868
  7.2 0.9 %copy-start.5 = (f32[256,256]{1,0:T(8,128)S(1)}, f32[256,256]{1,0:T(8,128)}, u32[]{:S(2)}) copy-start(f32[256,256]{1,0:T(8,128)} %phase_ref.1) | copy-start | bytes 786436
  8.2 52.4 %copy-start.6 = (f32[2,2,256,128]{3,2,1,0:T(8,128)S(1)}, f32[2,2,256,128]{3,2,1,0:T(8,128)}, u32[]{:S(2)}) copy-start(f32[2,2,256,128]{3,2,1,0:T(8,128)} %param.13) | copy-start | bytes 1572868

commit v2 on v1

--- a/solution.py
+++ b/solution.py
@@ -66,8 +66,8 @@
     return ar * br - ai * bi, ar * bi + ai * br
 
 
-def masks(sc_ref, p, n, odd):
-    r, c = sc_ref[p, 0], sc_ref[p, 1]
+def masks(start, p, n, odd):
+    r, c = start(p)
     h = n // 2
     rows = lax.broadcasted_iota(jnp.int32, (n, h), 0)
     cols = lax.broadcasted_iota(jnp.int32, (n, h), 1)
@@ -103,8 +103,8 @@
 
 
 def kernel(
-    sizes, sc_ref, own, probe_ref, phase_ref, intensity_hbm, right_hbm, left_hbm, out_ref,
-    right_ref, left_ref, intensity_ref, tr_ref, roll_ref, phi_ref, back_ref,
+    sizes, corner_ref, own_hbm, probe_hbm, phase_hbm, intensity_hbm, right_hbm, left_hbm, out_ref,
+    own, probe_ref, phase_ref, right_ref, left_ref, intensity_ref, tr_ref, roll_ref, phi_ref, back_ref,
     part, far, edge, g_tile, g_edge, rows_in, far_in, part_in,
     local_sem, m_send, m_recv, f_send, f_recv, e_send, e_recv,
     r_send, r_recv, gf_send, gf_recv, gp_send, gp_recv,
@@ -122,10 +122,20 @@
     has_up, has_down = iy > 0, iy < nty - 1
     vertical = ((iy - 1, has_up), (iy + 1, has_down))
 
+    def start(p):
+        return corner_ref[p, 0] - (iy * n - h), corner_ref[p, 1] - (ix * h - h)
+
     loads = [
         pltpu.make_async_copy(a, b, local_sem.at[i])
         for i, (a, b) in enumerate(
-            ((right_hbm, right_ref), (left_hbm, left_ref), (intensity_hbm, intensity_ref))
+            (
+                (own_hbm, own),
+                (phase_hbm, phase_ref),
+                (probe_hbm, probe_ref),
+                (right_hbm, right_ref),
+                (left_hbm, left_ref),
+                (intensity_hbm, intensity_ref),
+            )
         )
     ]
     for load in loads:
@@ -246,19 +256,23 @@
             part_copy(s, q, b).wait_recv()
             out_ref[s, q, half(b), :] = g_tile[s, 0, q, half(b), :] + part_in[s, q, half(b), :]
 
+    loads[0].wait()
     start_own(0)
     start_own_edges(0)
     start_own(1)
     start_own_edges(1)
+    loads[1].wait()
+    loads[2].wait()
     tr_ref[0] = jnp.cos(phase_ref[...])
     tr_ref[1] = jnp.sin(phase_ref[...])
     for p in range(count):
-        r, c = lax.rem(sc_ref[p, 0], n), sc_ref[p, 1]
+        r, c = start(p)
+        r = lax.rem(r, n)
         roll_ref[p, 0] = pltpu.roll(pltpu.roll(probe_ref[0], c, 1), r, 0)
         roll_ref[p, 1] = pltpu.roll(pltpu.roll(probe_ref[1], c, 1), r, 0)
     g_tile[...] = jnp.zeros_like(g_tile)
     g_edge[...] = jnp.zeros_like(g_edge)
-    for load in loads:
+    for load in loads[3:]:
         load.wait()
     on_swap(0)
     on_relay(0)
@@ -270,7 +284,7 @@
         def _():
             on_relay(1)
 
-        mask = masks(sc_ref, p, n, odd)
+        mask = masks(start, p, n, odd)
         tiles = (own.at[0], part.at[0], far.at[0])
         wr = window(0, tiles, edge.at[0], mask, n)
         wi = window(1, tiles, edge.at[0], mask, n)
@@ -286,7 +300,7 @@
     on_edges(1)
 
     def second(p, carry):
-        mask = masks(sc_ref, p, n, odd)
+        mask = masks(start, p, n, odd)
         tiles = (own.at[1], part.at[1], far.at[1])
         wr = window(0, tiles, edge.at[1], mask, n)
         wi = window(1, tiles, edge.at[1], mask, n)
@@ -305,7 +319,7 @@
     send_rows(1)
 
     def third(p, carry):
-        mask = masks(sc_ref, p, n, odd)
+        mask = masks(start, p, n, odd)
         xr, xi = fft2(back_ref[p, 0], back_ref[p, 1], right_ref, left_ref)
         xr, xi = mul(tr_ref[0], -tr_ref[1], xr, xi)
         back_ref[p, 0] = xr
@@ -359,8 +373,6 @@
     assert tile_rows == n and tile_cols == h
     nty, ntx = lax.axis_size("ty"), lax.axis_size("tx")
     assert ntx % 2 == 0
-    iy, ix = lax.axis_index("ty"), lax.axis_index("tx")
-    sc = jnp.stack([corner[:, 0] - (iy * tile_rows - h), corner[:, 1] - (ix * tile_cols - h)], axis=1)
     right, left = dft_tables(n)
     f32 = jnp.float32
     field = pltpu.VMEM((count, 2, n, n), f32)
@@ -369,9 +381,12 @@
     gradient = pl.pallas_call(
         functools.partial(kernel, (nty, ntx)),
         out_shape=jax.ShapeDtypeStruct(object_slices.shape, f32),
-        in_specs=[SMEM, VMEM, VMEM, VMEM, ANY, ANY, ANY],
+        in_specs=[SMEM] + [ANY] * 6,
         out_specs=VMEM,
         scratch_shapes=[
+            pltpu.VMEM(object_slices.shape, f32),
+            pltpu.VMEM(probe.shape, f32),
+            pltpu.VMEM(prop_phase.shape, f32),
             pltpu.VMEM(right.shape, right.dtype),
             pltpu.VMEM(left.shape, left.dtype),
             pltpu.VMEM(intensity.shape, f32),
@@ -387,15 +402,15 @@
             pltpu.VMEM(edges, f32),
             pltpu.VMEM(tiles, f32),
             pltpu.VMEM(tiles, f32),
-            dma((3,)),
+            dma((6,)),
         ]
         + [dma((2, 2, 2))] * 4
         + [dma((2, 2, 3, 2))] * 4
         + [dma((2, 2, 2))] * 4,
         compiler_params=pltpu.CompilerParams(
-            collective_id=0, has_side_effects=True, vmem_limit_bytes=48 << 20
+            collective_id=0, has_side_effects=True, vmem_limit_bytes=67043328
         ),
-    )(sc, object_slices, probe, prop_phase, intensity, right, left)
+    )(corner, object_slices, probe, prop_phase, intensity, right, left)
     momentum_next = decay_rate * momentum + grad_scale * gradient
     object_next = object_slices - step_length * momentum_next
     return (object_next, momentum_next)

time: 62.1 us -> 56.4 us (0.908)
  local copies, waits for them, and re-layouts: 6.62 us -> 0 us
  Pallas kernels: 52.4 us -> 53.1 us
    unnamed x14 -> x0, local copies, waits for them, and re-layouts: 6.62 us -> none
    sub x1, other arithmetic: 1.08 us -> 2.44 us  [on_device(): object_next = object_slices - step_length * momentum_next]
    sub x1 -> x0, other arithmetic: 0.83 us -> none  [on_device(): corner[:, 0] - (iy * tile_rows - h)]
    pallas_call x1, Pallas kernels: 52.4 us -> 53.1 us  [on_device(): pl.pallas_call(functools.partial(kernel, (nty, ntx)), out_shape=jax.Shape...]
where the time goes in v2:
time: 56.4 us; the launch traced here: 56.2 us
  Pallas kernels  53.1 us (94%)
  other arithmetic  2.44 us (4%)
  between operations  0.64 us (1%)
    pallas_call x1, Pallas kernels, on_device(): pl.pallas_call(functools.partial(kernel, (nty, ntx)), out_shape=jax.Shape...  53.1 us
    sub x1, other arithmetic, on_device(): object_next = object_slices - step_length * momentum_next  2.44 us

profile of v2, /device:TPU:6, one launch (start us, length us, event | category | flops | bytes accessed | tf_op | source)
XLA Modules:
  0.0 56.2 jit_solution(5753719342431160048)
XLA Ops:
  0.6 53.1 %shard_map.95 = f32[2,2,256,128]{3,2,1,0:T(8,128)} custom-call(s32[2,2]{1,0:T(2,128)} %corner_ref.1, f32[2,2,256,128]{3,2,1,0:T(8,128)} %own_hbm.1, f32[2,256,256]{2,1,0:T(8,128)} %probe_hbm.1, f32[256,256]{1,0:T(8,128)} %phase_hbm.1, f32[2,256,256]{2,1,0:T(8,128)} %intensity_hbm.1, bf16[1536,512]{1,0:T(8,128)(2,1)} %constant.10.clone.right_hbm, ...), custom_call_target="tpu_custom_call" | custom-call | tf_op jit(solution)/shard_map/pallas_call | solution.py:381
  53.8 2.4 %multiply_subtract_fusion = (f32[2,2,256,128]{3,2,1,0:T(8,128)}, f32[2,2,256,128]{3,2,1,0:T(8,128)}) fusion(f32[2,2,256,128]{3,2,1,0:T(8,128)} %own_hbm.1, f32[2,2,256,128]{3,2,1,0:T(8,128)} %shard_map.95, f32[2,2,256,128]{3,2,1,0:T(8,128)} %param.13), kind=kLoop, calls=%fused_computation | loop fusion | flops 655360 | bytes 2621440 | tf_op jit(solution)/shard_map/sub | solution.py:415

commit v3 on v2

--- a/solution.py
+++ b/solution.py
@@ -167,13 +167,13 @@
         return pl.ds(b * h, h)
 
     def swap_copy(s, q, b):
-        return remote(own.at[s, q, half(b)], part.at[s, q, half(b)], m_send.at[s, q, b], m_recv.at[s, q, b], (iy, partner))
+        return remote(own_hbm.at[s, q, half(b)], part.at[s, q, half(b)], m_send.at[s, q, b], m_recv.at[s, q, b], (iy, partner))
 
     def relay_copy(s, q, b):
         return remote(part.at[s, q, half(b)], far.at[s, q, half(b)], f_send.at[s, q, b], f_recv.at[s, q, b], (iy, target))
 
     def edge_copy(s, q, b, t):
-        src = (own, part, far)[t]
+        src = (own_hbm, part, far)[t]
         return remote(src.at[s, q, half(b)], edge.at[s, b, t, q], e_send.at[s, b, t, q], e_recv.at[s, b, t, q], (vertical[b][0], ix))
 
     def rows_copy(s, q, b, t):
@@ -256,7 +256,6 @@
             part_copy(s, q, b).wait_recv()
             out_ref[s, q, half(b), :] = g_tile[s, 0, q, half(b), :] + part_in[s, q, half(b), :]
 
-    loads[0].wait()
     start_own(0)
     start_own_edges(0)
     start_own(1)
@@ -272,7 +271,7 @@
         roll_ref[p, 1] = pltpu.roll(pltpu.roll(probe_ref[1], c, 1), r, 0)
     g_tile[...] = jnp.zeros_like(g_tile)
     g_edge[...] = jnp.zeros_like(g_edge)
-    for load in loads[3:]:
+    for load in (loads[0], *loads[3:]):
         load.wait()
     on_swap(0)
     on_relay(0)
@@ -319,30 +318,23 @@
     send_rows(1)
 
     def third(p, carry):
+        @pl.when(p == 1)
+        def _():
+            send_far(1)
+
         mask = masks(start, p, n, odd)
         xr, xi = fft2(back_ref[p, 0], back_ref[p, 1], right_ref, left_ref)
-        xr, xi = mul(tr_ref[0], -tr_ref[1], xr, xi)
-        back_ref[p, 0] = xr
-        back_ref[p, 1] = xi
-
-        @pl.when(p == 0)
-        def _():
-            send_far(1)
-
-        @pl.when(p == 1)
-        def _():
-            send_part(1)
-
-        xr, xi = ifft2(back_ref[p, 0], back_ref[p, 1], right_ref, left_ref)
+        xr, xi = ifft2(*mul(tr_ref[0], -tr_ref[1], xr, xi), right_ref, left_ref)
         gr, gi = mul(roll_ref[p, 0], -roll_ref[p, 1], xr, xi)
         scatter(gr, 0, g_tile.at[0], g_edge.at[0], mask, n)
         scatter(gi, 1, g_tile.at[0], g_edge.at[0], mask, n)
         return carry
 
     lax.fori_loop(0, count, third, 0)
+    send_rows(0)
     if count == 1:
-        send_part(1)
-    send_rows(0)
+        send_far(1)
+    send_part(1)
     send_far(0)
     send_part(0)
     finish(1)

time: 56.4 us -> 56 us (level)
  the two profiles are of different devices: /device:TPU:6 before, /device:TPU:0 now
where the time goes in v3:
time: 56 us; the launch traced here: 55.8 us
  Pallas kernels  52.7 us (94%)
  other arithmetic  2.44 us (4%)
  between operations  0.64 us (1%)
    pallas_call x1, Pallas kernels, on_device(): pl.pallas_call(functools.partial(kernel, (nty, ntx)), out_shape=jax.Shape...  52.7 us
    sub x1, other arithmetic, on_device(): object_next = object_slices - step_length * momentum_next  2.44 us

profile of v3, /device:TPU:0, one launch (start us, length us, event | category | flops | bytes accessed | tf_op | source)
XLA Modules:
  0.0 55.8 jit_solution(10272621585916399147)
XLA Ops:
  0.6 52.7 %shard_map.95 = f32[2,2,256,128]{3,2,1,0:T(8,128)} custom-call(s32[2,2]{1,0:T(2,128)} %corner_ref.1, f32[2,2,256,128]{3,2,1,0:T(8,128)} %own_hbm.1, f32[2,256,256]{2,1,0:T(8,128)} %probe_hbm.1, f32[256,256]{1,0:T(8,128)} %phase_hbm.1, f32[2,256,256]{2,1,0:T(8,128)} %intensity_hbm.1, bf16[1536,512]{1,0:T(8,128)(2,1)} %constant.10.clone.right_hbm, ...), custom_call_target="tpu_custom_call" | custom-call | tf_op jit(solution)/shard_map/pallas_call | solution.py:373
  53.4 2.4 %multiply_subtract_fusion = (f32[2,2,256,128]{3,2,1,0:T(8,128)}, f32[2,2,256,128]{3,2,1,0:T(8,128)}) fusion(f32[2,2,256,128]{3,2,1,0:T(8,128)} %own_hbm.1, f32[2,2,256,128]{3,2,1,0:T(8,128)} %shard_map.95, f32[2,2,256,128]{3,2,1,0:T(8,128)} %param.13), kind=kLoop, calls=%fused_computation | loop fusion | flops 655360 | bytes 2621440 | tf_op jit(solution)/shard_map/sub | solution.py:407

commit v4 on v3

--- a/solution.py
+++ b/solution.py
@@ -195,16 +195,16 @@
         for q, b in chunks:
             pl.when(vertical[b][1])(lambda q=q, b=b: edge_copy(s, q, b, 0).start())
 
-    def on_swap(s):
-        for q, b in chunks:
+    def on_swap(s, group):
+        for q, b in group:
             swap_copy(s, q, b).wait_recv()
             pl.when(has_target)(lambda q=q, b=b: relay_copy(s, q, b).start())
             pl.when(vertical[b][1])(lambda q=q, b=b: edge_copy(s, q, b, 1).start())
 
-    def on_relay(s):
+    def on_relay(s, group):
         @pl.when(has_source)
         def _():
-            for q, b in chunks:
+            for q, b in group:
                 relay_copy(s, q, b).wait_recv()
                 pl.when(vertical[b][1])(lambda q=q, b=b: edge_copy(s, q, b, 2).start())
 
@@ -273,29 +273,39 @@
     g_edge[...] = jnp.zeros_like(g_edge)
     for load in (loads[0], *loads[3:]):
         load.wait()
-    on_swap(0)
-    on_relay(0)
-    on_swap(1)
+    on_swap(0, chunks)
+    on_relay(0, chunks)
+    on_swap(1, chunks[:2])
     on_edges(0)
 
     def first(p, carry):
         @pl.when(p == 1)
         def _():
-            on_relay(1)
+            on_relay(1, chunks[:2])
 
         mask = masks(start, p, n, odd)
         tiles = (own.at[0], part.at[0], far.at[0])
         wr = window(0, tiles, edge.at[0], mask, n)
         wi = window(1, tiles, edge.at[0], mask, n)
         xr, xi = fft2(*mul(roll_ref[p, 0], roll_ref[p, 1], wr, wi), right_ref, left_ref)
-        xr, xi = ifft2(*mul(tr_ref[0], tr_ref[1], xr, xi), right_ref, left_ref)
+        xr, xi = mul(tr_ref[0], tr_ref[1], xr, xi)
+
+        @pl.when(p == 0)
+        def _():
+            on_swap(1, chunks[2:])
+
+        @pl.when(p == 1)
+        def _():
+            on_relay(1, chunks[2:])
+
+        xr, xi = ifft2(xr, xi, right_ref, left_ref)
         phi_ref[p, 0] = xr
         phi_ref[p, 1] = xi
         return carry
 
     lax.fori_loop(0, count, first, 0)
     if count == 1:
-        on_relay(1)
+        on_relay(1, chunks)
     on_edges(1)
 
     def second(p, carry):

time: 56 us -> 55.2 us (0.986)
  the two profiles are of different devices: /device:TPU:0 before, /device:TPU:6 now
where the time goes in v4:
time: 55.2 us; the launch traced here: 54.5 us
  Pallas kernels  51.4 us (93%)
  other arithmetic  2.44 us (4%)
  between operations  0.64 us (1%)
    pallas_call x1, Pallas kernels, on_device(): pl.pallas_call(functools.partial(kernel, (nty, ntx)), out_shape=jax.Shape...  51.4 us
    sub x1, other arithmetic, on_device(): object_next = object_slices - step_length * momentum_next  2.44 us

profile of v4, /device:TPU:6, one launch (start us, length us, event | category | flops | bytes accessed | tf_op | source)
XLA Modules:
  0.0 54.5 jit_solution(13689883390150353836)
XLA Ops:
  0.6 51.4 %shard_map.95 = f32[2,2,256,128]{3,2,1,0:T(8,128)} custom-call(s32[2,2]{1,0:T(2,128)} %corner_ref.1, f32[2,2,256,128]{3,2,1,0:T(8,128)} %own_hbm.1, f32[2,256,256]{2,1,0:T(8,128)} %probe_hbm.1, f32[256,256]{1,0:T(8,128)} %phase_hbm.1, f32[2,256,256]{2,1,0:T(8,128)} %intensity_hbm.1, bf16[1536,512]{1,0:T(8,128)(2,1)} %constant.10.clone.right_hbm, ...), custom_call_target="tpu_custom_call" | custom-call | tf_op jit(solution)/shard_map/pallas_call | solution.py:383
  52.0 2.4 %multiply_subtract_fusion = (f32[2,2,256,128]{3,2,1,0:T(8,128)}, f32[2,2,256,128]{3,2,1,0:T(8,128)}) fusion(f32[2,2,256,128]{3,2,1,0:T(8,128)} %own_hbm.1, f32[2,2,256,128]{3,2,1,0:T(8,128)} %shard_map.95, f32[2,2,256,128]{3,2,1,0:T(8,128)} %param.13), kind=kLoop, calls=%fused_computation | loop fusion | flops 655360 | bytes 2621440 | tf_op jit(solution)/shard_map/sub | solution.py:417
